TPU v7x, 128 devices: a whole 4x4x4 slice. The times are simulated.
128 devices in a mesh: gx: 16 (over z, y), gy: 8 (over x, core).
Axes of the slice: x: 4, y: 4, z: 4, core: 2. Of those that a mesh axis runs over, the one named last changes fastest.
Arguments:
- centers: float32 [3, 262144], P(None, ('gx', 'gy')), may hold values from -6 to 6
- tilt_angle: float32 [262144], P(('gx', 'gy')), may hold values from -3.140625 to 3.140625
- turn_angle: float32 [262144], P(('gx', 'gy')), may hold values from -3.140625 to 3.140625
- radius: float32 [262144], P(('gx', 'gy')), may hold values from 0.5 to 2
- mobility_perp: float32 [262144], P(('gx', 'gy')), may hold values from 0.3 to 3
- mobility_axial: float32 [262144], P(('gx', 'gy')), may hold values from 0.2 to 2
- mobility_rot: float32 [262144], P(('gx', 'gy')), may hold values from 0.3 to 3
- external_load: float32 [6, 262144], P(None, ('gx', 'gy')), may hold values from -60 to 60
- local_first: int32 [327680], P(('gx', 'gy')), may hold values from 0 to 2047, as said below
- local_second: int32 [327680], P(('gx', 'gy')), may hold values from 0 to 2047
- arc_first: float32 [327680], P(('gx', 'gy')), may hold values from -1 to 1
- arc_second: float32 [327680], P(('gx', 'gy')), may hold values from -1 to 1
- cross_mine: int32 [128, 4, 256], P(('gx', 'gy')), may hold values from 0 to 2047
- cross_slot: int32 [128, 4, 256], P(('gx', 'gy')), may hold values from 0 to 127
- cross_arc_own: float32 [128, 4, 256], P(('gx', 'gy')), may hold values from -1 to 1
- cross_arc_other: float32 [128, 4, 256], P(('gx', 'gy')), may hold values from -1 to 1
- cross_count: int32 [128, 4], P(('gx', 'gy')), may hold values from 0 to 256, as said below
- export_rows: int32 [128, 4, 128], P(('gx', 'gy')), may hold values from 0 to 2047
Outputs:
- velocity: float32 [6, 262144], P(None, ('gx', 'gy'))
- force_local: float32 [327680], P(('gx', 'gy'))
- force_cross: float32 [128, 4, 256], P(('gx', 'gy'))
Inputs may be any that keep to these rules, and one draw needn't show every extreme that they name: local_second never equals local_first of the same pair. Slots c < cross_count[k, d] are live, the others dead. A direction whose partner lies outside the mesh has count 0. In every draw some block holds 256 live pairs.
All inputs are finite; a program needn't handle non-finite values.
Results may differ from a plain program's by a relative error of at most 0.00002.
Values sent between devices are 32-bit elements; how exact they have to be, the bound alone decides.
A program may use at most 64 MiB of HBM per device.

v0:
```python
import jax
import jax.numpy as jnp
from jax import lax
from jax.sharding import PartitionSpec as P

step_time = 0.5
floor_gap = 0.25
tiny = 1e-06


def passed_along(shard, axis, by):
    devices = lax.axis_size(axis)
    pairs = [(i, i + by) for i in range(devices) if 0 <= i + by < devices]
    return lax.ppermute(shard, axis, pairs)


def tangent_of(polar, azimuth):
    lifted = jnp.sin(polar)
    return jnp.stack([lifted * jnp.cos(azimuth), lifted * jnp.sin(azimuth), jnp.cos(polar)])


def cross_product(left, right):
    return jnp.stack(
        [
            left[1] * right[2] - left[2] * right[1],
            left[2] * right[0] - left[0] * right[2],
            left[0] * right[1] - left[1] * right[0],
        ]
    )


def pair_terms(geo_first, geo_second, arc_one, arc_two, live_mask):
    lever_first = arc_one * tangent_of(geo_first[3], geo_first[4])
    lever_second = arc_two * tangent_of(geo_second[3], geo_second[4])
    apart = geo_first[:3] + lever_first - geo_second[:3] - lever_second
    spacing = jnp.sqrt(jnp.sum(apart * apart, axis=0))
    normal = apart / jnp.maximum(spacing, floor_gap) * live_mask
    jacobian = jnp.concatenate(
        [normal, cross_product(lever_first, normal), cross_product(lever_second, normal)], axis=0
    )
    clearance = (spacing - geo_first[5] - geo_second[5]) * live_mask
    return (jacobian, clearance)


def rate_of(jacobian, moving_first, moving_second):
    return (
        jnp.sum(jacobian[:3] * (moving_first[:3] - moving_second[:3]), axis=0)
        + jnp.sum(jacobian[3:6] * moving_first[3:], axis=0)
        - jnp.sum(jacobian[6:] * moving_second[3:], axis=0)
    )


def push_terms(jacobian, amount):
    return (amount * jacobian[:6], -amount * jnp.concatenate([jacobian[:3], jacobian[6:]], axis=0))


def apply_mobility(applied, tangent, perp, axial, rotary):
    force = applied[:3]
    along = jnp.sum(tangent * force, axis=0)
    return jnp.concatenate([perp * force + axial * along * tangent, rotary * applied[3:]], axis=0)


def toward_owner(blocks):
    across = lax.axis_size("gy")
    received = []
    for position, offset in enumerate((1, across + 1, across, across - 1)):
        received.append(passed_along(blocks[position], ("gx", "gy"), -offset))
    return jnp.stack(received)


def toward_partner(blocks):
    across = lax.axis_size("gy")
    received = []
    for position, offset in enumerate((1, across + 1, across, across - 1)):
        received.append(passed_along(blocks[position], ("gx", "gy"), offset))
    return jnp.stack(received)


def sum_pairs(first_term, second_term):
    return lax.psum((first_term, second_term), ("gx", "gy"))


def on_device(
    centers,
    tilt_angle,
    turn_angle,
    radius,
    mobility_perp,
    mobility_axial,
    mobility_rot,
    external_load,
    local_first,
    local_second,
    arc_first,
    arc_second,
    cross_mine,
    cross_slot,
    cross_arc_own,
    cross_arc_other,
    cross_count,
    export_rows,
):
    seg_rows = centers.shape[1]
    local_pairs = local_first.shape[0]
    blocks_cap = cross_mine.shape[2]
    export_cap = export_rows.shape[2]
    geometry = jnp.concatenate([centers, tilt_angle[None], turn_angle[None], radius[None]], axis=0)
    tangent = tangent_of(tilt_angle, turn_angle)
    exported = export_rows[0]
    export_flat = exported.reshape(-1)
    own_rows = cross_mine[0].reshape(-1)
    all_rows = jnp.concatenate([local_first, local_second, own_rows])
    slot_flat = (cross_slot[0] + (jnp.arange(4, dtype=jnp.int32) * export_cap)[:, None]).reshape(-1)
    live_mask = (
        (jnp.arange(blocks_cap, dtype=jnp.int32)[None, :] < cross_count[0][:, None])
        .astype(jnp.float32)
        .reshape(-1)
    )

    def picked(source):
        taken = jnp.take(source, all_rows, axis=1)
        return (
            taken[:, :local_pairs],
            taken[:, local_pairs : 2 * local_pairs],
            taken[:, 2 * local_pairs :],
        )

    def outgoing(source):
        return jnp.moveaxis(jnp.take(source, exported, axis=1), 1, 0)

    def incoming(blocks):
        flattened = jnp.moveaxis(blocks, 0, 1).reshape(blocks.shape[1], -1)
        return jnp.take(flattened, slot_flat, axis=1)

    def mobile(applied):
        return apply_mobility(applied, tangent, mobility_perp, mobility_axial, mobility_rot)

    drift = mobile(external_load)
    remote_geometry = incoming(toward_owner(outgoing(geometry)))
    geo_one, geo_two, geo_own = picked(geometry)
    jacobian_local, clearance_local = pair_terms(geo_one, geo_two, arc_first, arc_second, 1.0)
    jacobian_cross, clearance_cross = pair_terms(
        geo_own,
        remote_geometry,
        cross_arc_own[0].reshape(-1),
        cross_arc_other[0].reshape(-1),
        live_mask,
    )

    def spread(amount_local, amount_cross):
        local_one, local_two = push_terms(jacobian_local, amount_local)
        cross_one, cross_two = push_terms(jacobian_cross, amount_cross)
        slot_loads = jnp.zeros((6, 4 * export_cap), jnp.float32).at[:, slot_flat].add(cross_two)
        returned = toward_partner(jnp.moveaxis(slot_loads.reshape(6, 4, export_cap), 1, 0))
        pushes = jnp.concatenate([local_one, local_two, cross_one], axis=1)
        loads = jnp.zeros((6, seg_rows), jnp.float32).at[:, all_rows].add(pushes)
        return loads.at[:, export_flat].add(jnp.moveaxis(returned, 0, 1).reshape(6, -1))

    def rates(moving, remote_moving=None):
        remote_moving = incoming(toward_owner(outgoing(moving)))
        move_one, move_two, move_own = picked(moving)
        rate_local = rate_of(jacobian_local, move_one, move_two)
        rate_cross = rate_of(jacobian_cross, move_own, remote_moving)
        return (rate_local, rate_cross)

    drift_local, drift_cross = rates(drift, None)
    slope_local = clearance_local / step_time + drift_local
    slope_cross = clearance_cross / step_time + drift_cross
    top_first = jnp.sum(slope_local * slope_local) + jnp.sum(slope_cross * slope_cross)
    loads_first = spread(slope_local, slope_cross)
    moved_first = mobile(loads_first)
    curved_local, curved_cross = rates(moved_first)
    top_first, bottom_first = sum_pairs(
        top_first, jnp.sum(slope_local * curved_local) + jnp.sum(slope_cross * curved_cross)
    )
    step_first = top_first / (bottom_first + tiny)
    thrust_local = jnp.maximum(0.0, -step_first * slope_local)
    thrust_cross = jnp.maximum(0.0, -step_first * slope_cross)
    loads_second = spread(thrust_local, thrust_cross)
    moved_second = mobile(loads_second)
    moving_one = drift + moved_second
    top_second = jnp.sum(thrust_local * thrust_local) + jnp.sum(thrust_cross * thrust_cross)
    rate_local, rate_cross = rates(moving_one)
    next_local = clearance_local / step_time + rate_local
    next_cross = clearance_cross / step_time + rate_cross
    top_second, bottom_second = sum_pairs(
        top_second,
        jnp.sum(thrust_local * (next_local - slope_local))
        + jnp.sum(thrust_cross * (next_cross - slope_cross)),
    )
    step_second = top_second / (bottom_second + tiny)
    force_local = jnp.maximum(0.0, thrust_local - step_second * next_local)
    force_cross = jnp.maximum(0.0, thrust_cross - step_second * next_cross)
    velocity = drift + mobile(spread(force_local, force_cross))
    return (velocity, force_local, force_cross.reshape(1, 4, blocks_cap))


def solution(mesh):
    return jax.shard_map(
        on_device,
        mesh=mesh,
        in_specs=(
            P(None, ("gx", "gy")),
            P(("gx", "gy")),
            P(("gx", "gy")),
            P(("gx", "gy")),
            P(("gx", "gy")),
            P(("gx", "gy")),
            P(("gx", "gy")),
            P(None, ("gx", "gy")),
            P(("gx", "gy")),
            P(("gx", "gy")),
            P(("gx", "gy")),
            P(("gx", "gy")),
            P(("gx", "gy"), None, None),
            P(("gx", "gy"), None, None),
            P(("gx", "gy"), None, None),
            P(("gx", "gy"), None, None),
            P(("gx", "gy"), None),
            P(("gx", "gy"), None, None),
        ),
        out_specs=(P(None, ("gx", "gy")), P(("gx", "gy")), P(("gx", "gy"), None, None)),
        check_vma=False,
    )
```

profile of v0, /device:TPU:1, one launch (start us, length us, event | category | flops | bytes accessed | tf_op | source)
XLA Modules:
  0.0 529.1 jit_solution(2936644011537897512)
XLA Ops:
  11.4 3.3 collective-permute-start
  14.7 1.3 collective-permute-start.1
  16.0 1.3 collective-permute-start.2
  17.3 1.3 collective-permute-start.3
  19.2 1.9 collective-permute-start.4
  23.0 20.9 %gather_fusion.1 = f32[6144,6]{1,0:T(8,128)} fusion(f32[6,2048]{0,1:T(8,128)S(1)} %copy.319, s32[6144]{0:T(1024)S(1)} %fusion.33), kind=kCustom, calls=%fused_computation.3.clone | custom fusion | bytes 319488 | tf_op jit(solution)/shard_map/jit(_take)/gather | solution.py:121
  43.9 20.9 %gather_fusion = f32[6144,6]{1,0:T(8,128)} fusion(f32[6,2048]{0,1:T(8,128)S(1)} %copy.317, s32[6144]{0:T(1024)S(1)} %fusion.33), kind=kCustom, calls=%fused_computation.clone | custom fusion | bytes 319488 | tf_op jit(solution)/shard_map/jit(_take)/gather | solution.py:121
  66.0 2.4 copy.320
  72.4 1.9 slice_reduce_fusion.1
  75.3 1.3 reshape_dynamic-update-slice_fusion
  88.5 3.3 gather_fusion.3
  92.7 1.6 collective-permute-done.7
  94.6 2.8 gather_fusion.5
  100.2 6.1 %scatter_custom_fusion.1 = f32[6,512]{0,1:T(8,128)S(1)} fusion(s32[1024]{0:T(1024)S(1)} %bitcast.296, f32[1024,6]{1,0:T(8,128)S(1)} %copy.336, f32[]{:T(128)} %constant.32.clone.1), kind=kCustom, calls=%fused_computation.39 | custom fusion | flops 6144 | bytes 12292 | tf_op jit(solution)/shard_map/scatter-add | solution.py:153
  106.4 4.1 collective-permute-start.8
  110.4 5.0 collective-permute-start.9
  115.5 5.1 collective-permute-start.10
  120.6 6.2 %collective-permute-start.11 = (f32[6,128]{1,0:T(8,128)S(1)}, f32[6,128]{1,0:T(8,128)S(1)}, u32[]{:S(2)}, u32[]{:S(2)}) collective-permute-start(f32[6,128]{1,0:T(8,128)S(1)} %get-tuple-element.130), channel_id=1, source_target_pairs={{0,7},{1,8},{2,9},{3,10},{4,11},{5,12},{6,13},{7,14},{8,15},{9,16}... | collective-permute-start | bytes 9224 | tf_op jit(solution)/shard_map/ppermute | solution.py:14
  128.0 2.2 copy.335
  130.8 33.7 %scatter_custom_fusion = f32[6,2048]{0,1:T(8,128)S(1)} fusion(s32[6144]{0:T(1024)S(1)} %bitcast.275, f32[6144,6]{1,0:T(8,128)} %copy.335, f32[]{:T(128)} %constant.32.clone.1), kind=kCustom, calls=%fused_computation.25 | custom fusion | flops 36864 | bytes 49664 | tf_op jit(solution)/shard_map/scatter-add | solution.py:156
  164.9 4.2 scatter_fusion
  171.8 20.9 %gather_fusion.6 = f32[6144,6]{1,0:T(8,128)} fusion(f32[6,2048]{0,1:T(8,128)S(1)} %copy.344, s32[6144]{0:T(1024)S(1)} %copy-done.4), kind=kCustom, calls=%fused_computation.4.clone | custom fusion | bytes 319488 | tf_op jit(solution)/shard_map/jit(_take)/gather | solution.py:121
  192.9 3.2 collective-permute-start.12
  200.0 2.4 copy.345
  204.3 4.1 collective-permute-done.15
  208.6 2.8 gather_fusion.8
  215.5 74.8 %all-reduce.1 = (f32[]{:T(128)}, f32[]{:T(128)}) all-reduce(f32[]{:T(128)S(6)} %add.310, f32[]{:T(128)S(6)} %add.319), channel_id=1, replica_groups=mesh['gx'=16,'gy'=8] {'gx','gy'}, use_global_device_ids=true, to_apply=%region_11.15 | all-reduce | flops 2 | bytes 16 | tf_op jit(solution)/shard_map/psum | solution.py:80
  291.9 6.2 %scatter_custom_fusion.4 = f32[6,512]{0,1:T(8,128)S(1)} fusion(s32[1024]{0:T(1024)} %bitcast.297, f32[1024,6]{1,0:T(8,128)S(1)} %copy.354, f32[]{:T(128)} %constant.32.clone.1), kind=kCustom, calls=%fused_computation.37 | custom fusion | flops 6144 | bytes 12800 | tf_op jit(solution)/shard_map/scatter-add | solution.py:153
  298.2 3.8 collective-permute-start.16
  303.4 3.1 collective-permute-start.18
  306.5 2.8 collective-permute-start.19
  309.6 2.2 copy.353
  311.8 33.7 %scatter_custom_fusion.3 = f32[6,2048]{0,1:T(8,128)S(1)} fusion(s32[6144]{0:T(1024)} %bitcast.276, f32[6144,6]{1,0:T(8,128)} %copy.353, f32[]{:T(128)} %constant.32.clone.1), kind=kCustom, calls=%fused_computation.23 | custom fusion | flops 36864 | bytes 49664 | tf_op jit(solution)/shard_map/scatter-add | solution.py:156
  345.8 3.9 scatter_fusion.1
  351.4 20.9 %gather_fusion.9 = f32[6144,6]{1,0:T(8,128)} fusion(f32[6,2048]{0,1:T(8,128)S(1)} %copy.362, s32[6144]{0:T(1024)S(1)} %copy-done.4), kind=kCustom, calls=%fused_computation.5.clone | custom fusion | bytes 319488 | tf_op jit(solution)/shard_map/jit(_take)/gather | solution.py:121
  373.6 2.4 copy.363
  376.3 4.9 collective-permute-start.20
  387.1 3.7 collective-permute-done.23
  391.0 2.8 gather_fusion.11
  397.4 68.4 %all-reduce = (f32[]{:T(128)}, f32[]{:T(128)}) all-reduce(f32[]{:T(128)S(6)} %add.321, f32[]{:T(128)S(6)} %add.328), channel_id=1, replica_groups=mesh['gx'=16,'gy'=8] {'gx','gy'}, use_global_device_ids=true, to_apply=%region_27.31 | all-reduce | flops 2 | bytes 16 | tf_op jit(solution)/shard_map/psum | solution.py:80
  468.0 6.2 %scatter_custom_fusion.7 = f32[6,512]{0,1:T(8,128)S(1)} fusion(s32[1024]{0:T(1024)} %bitcast.298, f32[1024,6]{1,0:T(8,128)S(1)} %copy.372, f32[]{:T(128)} %constant.32.clone.1), kind=kCustom, calls=%fused_computation.35 | custom fusion | flops 6144 | bytes 12800 | tf_op jit(solution)/shard_map/scatter-add | solution.py:153
  474.4 1.9 collective-permute-start.24
  476.3 2.4 collective-permute-start.25
  478.7 2.2 collective-permute-start.26
  480.9 5.0 collective-permute-start.27
  486.9 2.2 copy.371
  489.1 33.7 %scatter_custom_fusion.6 = f32[6,2048]{0,1:T(8,128)S(1)} fusion(s32[6144]{0:T(1024)} %bitcast.277, f32[6144,6]{1,0:T(8,128)} %copy.371, f32[]{:T(128)} %constant.32.clone.1), kind=kCustom, calls=%fused_computation.21 | custom fusion | flops 36864 | bytes 49664 | tf_op jit(solution)/shard_map/scatter-add | solution.py:156
  523.1 3.9 scatter_fusion.2
  (379 shorter events, 62.8 us)
Async XLA Ops:
  2.1 62.7 %copy-start.73 = (pred[4,128]{1,0:T(4,128)(4,1)}, pred[4,128]{1,0:T(4,128)(4,1)S(1)}, u32[]{:S(2)}) copy-start(pred[4,128]{1,0:T(4,128)(4,1)S(1)} %compare_and_fusion.2) | copy-start | bytes 1540
  7.2 58.2 %copy-start.56 = (s32[1024]{0:T(1024)}, s32[1024]{0:T(1024)S(1)}, u32[]{:S(2)}) copy-start(s32[1024]{0:T(1024)S(1)} %pad_clamp_fusion) | copy-start | bytes 12292
  11.4 70.4 %collective-permute-start = (f32[6,128]{1,0:T(8,128)}, f32[6,128]{1,0:T(8,128)}, u32[]{:S(2)}, u32[]{:S(2)}) collective-permute-start(f32[6,128]{1,0:T(8,128)} %get-tuple-element.141), channel_id=1, source_target_pairs={{1,0},{2,1},{3,2},{4,3},{5,4},{6,5},{7,6},{8,7},{9,8},{10,9},{11,1... | collective-permute-start | bytes 9224 | tf_op jit(solution)/shard_map/ppermute | solution.py:14
  14.7 69.1 %collective-permute-start.1 = (f32[6,128]{1,0:T(8,128)}, f32[6,128]{1,0:T(8,128)}, u32[]{:S(2)}, u32[]{:S(2)}) collective-permute-start(f32[6,128]{1,0:T(8,128)} %get-tuple-element.144), channel_id=1, source_target_pairs={{9,0},{10,1},{11,2},{12,3},{13,4},{14,5},{15,6},{16,7},{17,8},{18,... | collective-permute-start | bytes 9224 | tf_op jit(solution)/shard_map/ppermute | solution.py:14
  16.0 69.7 %collective-permute-start.2 = (f32[6,128]{1,0:T(8,128)}, f32[6,128]{1,0:T(8,128)}, u32[]{:S(2)}, u32[]{:S(2)}) collective-permute-start(f32[6,128]{1,0:T(8,128)} %get-tuple-element.143), channel_id=1, source_target_pairs={{8,0},{9,1},{10,2},{11,3},{12,4},{13,5},{14,6},{15,7},{16,8},{17,9... | collective-permute-start | bytes 9224 | tf_op jit(solution)/shard_map/ppermute | solution.py:14
  17.3 70.4 %collective-permute-start.3 = (f32[6,128]{1,0:T(8,128)}, f32[6,128]{1,0:T(8,128)}, u32[]{:S(2)}, u32[]{:S(2)}) collective-permute-start(f32[6,128]{1,0:T(8,128)} %get-tuple-element.142), channel_id=1, source_target_pairs={{7,0},{8,1},{9,2},{10,3},{11,4},{12,5},{13,6},{14,7},{15,8},{16,9}... | collective-permute-start | bytes 9224 | tf_op jit(solution)/shard_map/ppermute | solution.py:14
  19.2 72.9 %collective-permute-start.4 = (f32[6,128]{1,0:T(8,128)}, f32[6,128]{1,0:T(8,128)}, u32[]{:S(2)}, u32[]{:S(2)}) collective-permute-start(f32[6,128]{1,0:T(8,128)} %get-tuple-element.137), channel_id=1, source_target_pairs={{1,0},{2,1},{3,2},{4,3},{5,4},{6,5},{7,6},{8,7},{9,8},{10,9},{11,1... | collective-permute-start | bytes 9224 | tf_op jit(solution)/shard_map/ppermute | solution.py:14
  78.7 52.1 %copy-start.61 = (s32[6144,1]{0,1:T(1,128)}, s32[6144,1]{0,1:T(1,128)S(1)}, u32[]{:S(2)}) copy-start(s32[6144,1]{0,1:T(1,128)S(1)} %compare_select_fusion) | copy-start | bytes 73732
  78.7 51.5 %copy-start.76 = (s32[1024,1]{0,1:T(1,128)}, s32[1024,1]{0,1:T(1,128)S(1)}, u32[]{:S(2)}) copy-start(s32[1024,1]{0,1:T(1,128)S(1)} %compare_select_fusion.2) | copy-start | bytes 12292
  80.3 84.6 %copy-start.58 = (s32[512,1]{0,1:T(1,128)}, s32[512,1]{0,1:T(1,128)S(1)}, u32[]{:S(2)}) copy-start(s32[512,1]{0,1:T(1,128)S(1)} %compare_select_fusion.3) | copy-start | bytes 6148
  81.7 48.5 %copy-start.38 = (f32[1,2,4,128]{3,1,2,0:T(2,128)}, f32[1,2,4,128]{3,1,2,0:T(2,128)S(1)}, u32[]{:S(2)}) copy-start(f32[1,2,4,128]{3,1,2,0:T(2,128)S(1)} %copy.396) | copy-start | bytes 12292
  81.7 11.0 %collective-permute-start.5 = (f32[6,128]{1,0:T(8,128)}, f32[6,128]{1,0:T(8,128)S(1)}, u32[]{:S(2)}, u32[]{:S(2)}) collective-permute-start(f32[6,128]{1,0:T(8,128)} %get-tuple-element.140), channel_id=1, source_target_pairs={{9,0},{10,1},{11,2},{12,3},{13,4},{14,5},{15,6},{16,7},{17,8},{18,... | collective-permute-start | bytes 9224 | tf_op jit(solution)/shard_map/ppermute | solution.py:14
  83.7 9.0 %collective-permute-start.6 = (f32[6,128]{1,0:T(8,128)}, f32[6,128]{1,0:T(8,128)S(1)}, u32[]{:S(2)}, u32[]{:S(2)}) collective-permute-start(f32[6,128]{1,0:T(8,128)} %get-tuple-element.139), channel_id=1, source_target_pairs={{8,0},{9,1},{10,2},{11,3},{12,4},{13,5},{14,6},{15,7},{16,8},{17,9... | collective-permute-start | bytes 9224 | tf_op jit(solution)/shard_map/ppermute | solution.py:14
  85.7 8.7 %collective-permute-start.7 = (f32[6,128]{1,0:T(8,128)}, f32[6,128]{1,0:T(8,128)S(1)}, u32[]{:S(2)}, u32[]{:S(2)}) collective-permute-start(f32[6,128]{1,0:T(8,128)} %get-tuple-element.138), channel_id=1, source_target_pairs={{7,0},{8,1},{9,2},{10,3},{11,4},{12,5},{13,6},{14,7},{15,8},{16,9}... | collective-permute-start | bytes 9224 | tf_op jit(solution)/shard_map/ppermute | solution.py:14
  98.8 65.8 %copy-start.9 = (f32[1,1024]{1,0:T(1,128)}, f32[1,1024]{1,0:T(1,128)S(1)}, u32[]{:S(2)}) copy-start(f32[1,1024]{1,0:T(1,128)S(1)} %get-tuple-element.106) | copy-start | bytes 12292
  98.8 65.8 %copy-start.12 = (f32[1,1024]{1,0:T(1,128)}, f32[1,1024]{1,0:T(1,128)S(1)}, u32[]{:S(2)}) copy-start(f32[1,1024]{1,0:T(1,128)S(1)} %get-tuple-element.107) | copy-start | bytes 12292
  98.8 65.8 %copy-start.15 = (f32[1,1024]{1,0:T(1,128)}, f32[1,1024]{1,0:T(1,128)S(1)}, u32[]{:S(2)}) copy-start(f32[1,1024]{1,0:T(1,128)S(1)} %get-tuple-element.108) | copy-start | bytes 12292
  106.4 58.2 %collective-permute-start.8 = (f32[6,128]{1,0:T(8,128)S(1)}, f32[6,128]{1,0:T(8,128)S(1)}, u32[]{:S(2)}, u32[]{:S(2)}) collective-permute-start(f32[6,128]{1,0:T(8,128)S(1)} %get-tuple-element.129), channel_id=1, source_target_pairs={{0,1},{1,2},{2,3},{3,4},{4,5},{5,6},{6,7},{7,8},{8,9},{9,10},{10,1... | collective-permute-start | bytes 9224 | tf_op jit(solution)/shard_map/ppermute | solution.py:14
  110.4 54.2 %collective-permute-start.9 = (f32[6,128]{1,0:T(8,128)S(1)}, f32[6,128]{1,0:T(8,128)S(1)}, u32[]{:S(2)}, u32[]{:S(2)}) collective-permute-start(f32[6,128]{1,0:T(8,128)S(1)} %get-tuple-element.132), channel_id=1, source_target_pairs={{0,9},{1,10},{2,11},{3,12},{4,13},{5,14},{6,15},{7,16},{8,17},{9,1... | collective-permute-start | bytes 9224 | tf_op jit(solution)/shard_map/ppermute | solution.py:14
  115.5 49.2 %collective-permute-start.10 = (f32[6,128]{1,0:T(8,128)S(1)}, f32[6,128]{1,0:T(8,128)S(1)}, u32[]{:S(2)}, u32[]{:S(2)}) collective-permute-start(f32[6,128]{1,0:T(8,128)S(1)} %get-tuple-element.131), channel_id=1, source_target_pairs={{0,8},{1,9},{2,10},{3,11},{4,12},{5,13},{6,14},{7,15},{8,16},{9,17... | collective-permute-start | bytes 9224 | tf_op jit(solution)/shard_map/ppermute | solution.py:14
  120.6 44.1 %collective-permute-start.11 = (f32[6,128]{1,0:T(8,128)S(1)}, f32[6,128]{1,0:T(8,128)S(1)}, u32[]{:S(2)}, u32[]{:S(2)}) collective-permute-start(f32[6,128]{1,0:T(8,128)S(1)} %get-tuple-element.130), channel_id=1, source_target_pairs={{0,7},{1,8},{2,9},{3,10},{4,11},{5,12},{6,13},{7,14},{8,15},{9,16}... | collective-permute-start | bytes 9224 | tf_op jit(solution)/shard_map/ppermute | solution.py:14
  192.9 11.0 %collective-permute-start.12 = (f32[6,128]{1,0:T(8,128)S(1)}, f32[6,128]{1,0:T(8,128)S(1)}, u32[]{:S(2)}, u32[]{:S(2)}) collective-permute-start(f32[6,128]{1,0:T(8,128)S(1)} %get-tuple-element.125), channel_id=1, source_target_pairs={{1,0},{2,1},{3,2},{4,3},{5,4},{6,5},{7,6},{8,7},{9,8},{10,9},{11,1... | collective-permute-start | bytes 9224 | tf_op jit(solution)/shard_map/ppermute | solution.py:14
  196.1 7.8 %collective-permute-start.13 = (f32[6,128]{1,0:T(8,128)S(1)}, f32[6,128]{1,0:T(8,128)S(1)}, u32[]{:S(2)}, u32[]{:S(2)}) collective-permute-start(f32[6,128]{1,0:T(8,128)S(1)} %get-tuple-element.128), channel_id=1, source_target_pairs={{9,0},{10,1},{11,2},{12,3},{13,4},{14,5},{15,6},{16,7},{17,8},{18,... | collective-permute-start | bytes 9224 | tf_op jit(solution)/shard_map/ppermute | solution.py:14
  197.4 6.9 %collective-permute-start.14 = (f32[6,128]{1,0:T(8,128)S(1)}, f32[6,128]{1,0:T(8,128)S(1)}, u32[]{:S(2)}, u32[]{:S(2)}) collective-permute-start(f32[6,128]{1,0:T(8,128)S(1)} %get-tuple-element.127), channel_id=1, source_target_pairs={{8,0},{9,1},{10,2},{11,3},{12,4},{13,5},{14,6},{15,7},{16,8},{17,9... | collective-permute-start | bytes 9224 | tf_op jit(solution)/shard_map/ppermute | solution.py:14
  198.7 110.7 %copy-start.49 = (f32[1,2560]{1,0:T(1,128)S(1)}, f32[1,2560]{1,0:T(1,128)}, u32[]{:S(2)}) copy-start(f32[1,2560]{1,0:T(1,128)} %get-tuple-element.61) | copy-start | bytes 30724
  198.7 9.7 %collective-permute-start.15 = (f32[6,128]{1,0:T(8,128)S(1)}, f32[6,128]{1,0:T(8,128)S(1)}, u32[]{:S(2)}, u32[]{:S(2)}) collective-permute-start(f32[6,128]{1,0:T(8,128)S(1)} %get-tuple-element.126), channel_id=1, source_target_pairs={{7,0},{8,1},{9,2},{10,3},{11,4},{12,5},{13,6},{14,7},{15,8},{16,9}... | collective-permute-start | bytes 9224 | tf_op jit(solution)/shard_map/ppermute | solution.py:14
  291.9 53.9 %copy-start.59 = (s32[512,1]{0,1:T(1,128)S(1)}, s32[512,1]{0,1:T(1,128)}, u32[]{:S(2)}) copy-start(s32[512,1]{0,1:T(1,128)} %copy-done.58) | copy-start | bytes 6148
  298.2 47.3 %collective-permute-start.16 = (f32[6,128]{1,0:T(8,128)S(1)}, f32[6,128]{1,0:T(8,128)S(1)}, u32[]{:S(2)}, u32[]{:S(2)}) collective-permute-start(f32[6,128]{1,0:T(8,128)S(1)} %get-tuple-element.119), channel_id=1, source_target_pairs={{0,1},{1,2},{2,3},{3,4},{4,5},{5,6},{6,7},{7,8},{8,9},{9,10},{10,1... | collective-permute-start | bytes 9224 | tf_op jit(solution)/shard_map/ppermute | solution.py:14
  302.1 43.5 %collective-permute-start.17 = (f32[6,128]{1,0:T(8,128)S(1)}, f32[6,128]{1,0:T(8,128)S(1)}, u32[]{:S(2)}, u32[]{:S(2)}) collective-permute-start(f32[6,128]{1,0:T(8,128)S(1)} %get-tuple-element.122), channel_id=1, source_target_pairs={{0,9},{1,10},{2,11},{3,12},{4,13},{5,14},{6,15},{7,16},{8,17},{9,1... | collective-permute-start | bytes 9224 | tf_op jit(solution)/shard_map/ppermute | solution.py:14
  303.4 42.2 %collective-permute-start.18 = (f32[6,128]{1,0:T(8,128)S(1)}, f32[6,128]{1,0:T(8,128)S(1)}, u32[]{:S(2)}, u32[]{:S(2)}) collective-permute-start(f32[6,128]{1,0:T(8,128)S(1)} %get-tuple-element.121), channel_id=1, source_target_pairs={{0,8},{1,9},{2,10},{3,11},{4,12},{5,13},{6,14},{7,15},{8,16},{9,17... | collective-permute-start | bytes 9224 | tf_op jit(solution)/shard_map/ppermute | solution.py:14
  306.5 39.1 %collective-permute-start.19 = (f32[6,128]{1,0:T(8,128)S(1)}, f32[6,128]{1,0:T(8,128)S(1)}, u32[]{:S(2)}, u32[]{:S(2)}) collective-permute-start(f32[6,128]{1,0:T(8,128)S(1)} %get-tuple-element.120), channel_id=1, source_target_pairs={{0,7},{1,8},{2,9},{3,10},{4,11},{5,12},{6,13},{7,14},{8,15},{9,16}... | collective-permute-start | bytes 9224 | tf_op jit(solution)/shard_map/ppermute | solution.py:14
  351.4 39.6 %copy-start.37 = (s32[1024]{0:T(1024)S(1)}, s32[1024]{0:T(1024)}, u32[]{:S(2)}) copy-start(s32[1024]{0:T(1024)} %broadcast_clamp_fusion) | copy-start | bytes 12292
  373.5 112.4 %copy-start.50 = (f32[1,2560]{1,0:T(1,128)S(1)}, f32[1,2560]{1,0:T(1,128)}, u32[]{:S(2)}) copy-start(f32[1,2560]{1,0:T(1,128)} %get-tuple-element.61) | copy-start | bytes 30724
  373.5 112.4 %copy-start.55 = (f32[1,2560]{1,0:T(1,128)S(1)}, f32[1,2560]{1,0:T(1,128)}, u32[]{:S(2)}) copy-start(f32[1,2560]{1,0:T(1,128)} %get-tuple-element.62) | copy-start | bytes 30724
  375.9 110.2 %copy-start.66 = (f32[1,4,256]{2,1,0:T(4,128)S(1)}, f32[1,4,256]{2,1,0:T(4,128)}, u32[]{:S(2)}) copy-start(f32[1,4,256]{2,1,0:T(4,128)} %sub.334) | copy-start | bytes 12292
  375.9 110.2 %copy-start.67 = (f32[1,4,256]{2,1,0:T(4,128)S(1)}, f32[1,4,256]{2,1,0:T(4,128)}, u32[]{:S(2)}) copy-start(f32[1,4,256]{2,1,0:T(4,128)} %sqrt.64) | copy-start | bytes 12292
  376.0 110.2 %copy-start.68 = (f32[1,4,256]{2,1,0:T(4,128)S(1)}, f32[1,4,256]{2,1,0:T(4,128)}, u32[]{:S(2)}) copy-start(f32[1,4,256]{2,1,0:T(4,128)} %squeeze.193) | copy-start | bytes 12292
  376.0 110.2 %copy-start.69 = (f32[1,4,256]{2,1,0:T(4,128)S(1)}, f32[1,4,256]{2,1,0:T(4,128)}, u32[]{:S(2)}) copy-start(f32[1,4,256]{2,1,0:T(4,128)} %squeeze.194) | copy-start | bytes 12292
  376.0 110.2 %copy-start.77 = (s32[1,4]{1,0:T(1,128)S(1)}, s32[1,4]{1,0:T(1,128)}, u32[]{:S(2)}) copy-start(s32[1,4]{1,0:T(1,128)} %param.40) | copy-start | bytes 52
  376.3 9.5 %collective-permute-start.20 = (f32[6,128]{1,0:T(8,128)S(1)}, f32[6,128]{1,0:T(8,128)S(1)}, u32[]{:S(2)}, u32[]{:S(2)}) collective-permute-start(f32[6,128]{1,0:T(8,128)S(1)} %get-tuple-element.115), channel_id=1, source_target_pairs={{1,0},{2,1},{3,2},{4,3},{5,4},{6,5},{7,6},{8,7},{9,8},{10,9},{11,1... | collective-permute-start | bytes 9224 | tf_op jit(solution)/shard_map/ppermute | solution.py:14
  381.3 5.8 %collective-permute-start.21 = (f32[6,128]{1,0:T(8,128)S(1)}, f32[6,128]{1,0:T(8,128)S(1)}, u32[]{:S(2)}, u32[]{:S(2)}) collective-permute-start(f32[6,128]{1,0:T(8,128)S(1)} %get-tuple-element.118), channel_id=1, source_target_pairs={{9,0},{10,1},{11,2},{12,3},{13,4},{14,5},{15,6},{16,7},{17,8},{18,... | collective-permute-start | bytes 9224 | tf_op jit(solution)/shard_map/ppermute | solution.py:14
  382.6 4.5 collective-permute-start.22
  383.9 6.9 %collective-permute-start.23 = (f32[6,128]{1,0:T(8,128)S(1)}, f32[6,128]{1,0:T(8,128)S(1)}, u32[]{:S(2)}, u32[]{:S(2)}) collective-permute-start(f32[6,128]{1,0:T(8,128)S(1)} %get-tuple-element.116), channel_id=1, source_target_pairs={{7,0},{8,1},{9,2},{10,3},{11,4},{12,5},{13,6},{14,7},{15,8},{16,9}... | collective-permute-start | bytes 9224 | tf_op jit(solution)/shard_map/ppermute | solution.py:14
  468.0 55.1 %copy-start.60 = (s32[512,1]{0,1:T(1,128)S(1)}, s32[512,1]{0,1:T(1,128)}, u32[]{:S(2)}) copy-start(s32[512,1]{0,1:T(1,128)} %copy-done.58) | copy-start | bytes 6148
  474.4 48.5 %collective-permute-start.24 = (f32[6,128]{1,0:T(8,128)S(1)}, f32[6,128]{1,0:T(8,128)S(1)}, u32[]{:S(2)}, u32[]{:S(2)}) collective-permute-start(f32[6,128]{1,0:T(8,128)S(1)} %get-tuple-element.109), channel_id=1, source_target_pairs={{0,1},{1,2},{2,3},{3,4},{4,5},{5,6},{6,7},{7,8},{8,9},{9,10},{10,1... | collective-permute-start | bytes 9224 | tf_op jit(solution)/shard_map/ppermute | solution.py:14
  476.3 46.5 %collective-permute-start.25 = (f32[6,128]{1,0:T(8,128)S(1)}, f32[6,128]{1,0:T(8,128)S(1)}, u32[]{:S(2)}, u32[]{:S(2)}) collective-permute-start(f32[6,128]{1,0:T(8,128)S(1)} %get-tuple-element.112), channel_id=1, source_target_pairs={{0,9},{1,10},{2,11},{3,12},{4,13},{5,14},{6,15},{7,16},{8,17},{9,1... | collective-permute-start | bytes 9224 | tf_op jit(solution)/shard_map/ppermute | solution.py:14
  478.7 44.2 %collective-permute-start.26 = (f32[6,128]{1,0:T(8,128)S(1)}, f32[6,128]{1,0:T(8,128)S(1)}, u32[]{:S(2)}, u32[]{:S(2)}) collective-permute-start(f32[6,128]{1,0:T(8,128)S(1)} %get-tuple-element.111), channel_id=1, source_target_pairs={{0,8},{1,9},{2,10},{3,11},{4,12},{5,13},{6,14},{7,15},{8,16},{9,17... | collective-permute-start | bytes 9224 | tf_op jit(solution)/shard_map/ppermute | solution.py:14
  480.9 42.0 %collective-permute-start.27 = (f32[6,128]{1,0:T(8,128)S(1)}, f32[6,128]{1,0:T(8,128)S(1)}, u32[]{:S(2)}, u32[]{:S(2)}) collective-permute-start(f32[6,128]{1,0:T(8,128)S(1)} %get-tuple-element.110), channel_id=1, source_target_pairs={{0,7},{1,8},{2,9},{3,10},{4,11},{5,12},{6,13},{7,14},{8,15},{9,16}... | collective-permute-start | bytes 9224 | tf_op jit(solution)/shard_map/ppermute | solution.py:14
  (58 other events, 1008.9 us)
where the time goes:
time: 539 us; the launch traced here: 529 us
  other arithmetic  154 us (29%)
  blocking collectives  143 us (27%)
  local copies, waits for them, and re-layouts  138 us (26%)
  starting transfers between devices  71.9 us (13%)
  waiting for transfers between devices  11.1 us (2%)
  between operations  10.8 us (2%)
    psum x2, blocking collectives, sum_pairs(): return lax.psum((first_term, second_term), ('gx', 'gy'))  143 us
    scatter-add x3, other arithmetic, spread(): loads = jnp.zeros((6, seg_rows), jnp.float32).at[:, all_rows].add(pushes)  101 us
    gather x8, local copies, waits for them, and re-layouts, picked(): taken = jnp.take(source, all_rows, axis=1)  91.8 us
    ppermute x28, starting transfers between devices, passed_along(): return lax.ppermute(shard, axis, pairs)  71.9 us
    scatter-add x3, other arithmetic, spread(): jnp.zeros((6, 4 * export_cap), jnp.float32).at[:, slot_flat].add(cross_two)  18.5 us
    gather x8, local copies, waits for them, and re-layouts, incoming(): return jnp.take(flattened, slot_flat, axis=1)  12.5 us
    scatter-add x3, other arithmetic, spread(): loads.at[:, export_flat].add(jnp.moveaxis(returned, 0, 1).reshape(6, -1))  11.9 us
    ppermute x28, waiting for transfers between devices, passed_along(): return lax.ppermute(shard, axis, pairs)  11.1 us
  transfers between devices with their start and end apart: 28, of which 5 were waited for; matrix products, arithmetic and copies ran while one was open for 35% of the time, Pallas kernels for 0%

commit v1 on v0

--- a/solution.py
+++ b/solution.py
@@ -77,7 +77,7 @@
 
 
 def sum_pairs(first_term, second_term):
-    return lax.psum((first_term, second_term), ("gx", "gy"))
+    return lax.psum(lax.psum((first_term, second_term), "gy"), "gx")
 
 
 def on_device(

time: 539 us -> 497 us (0.922); the launches traced: 529 us -> 494 us
  blocking collectives: 143 us -> 105 us
    psum x2 -> x4, blocking collectives: 143 us -> 105 us  [sum_pairs(): return lax.psum(lax.psum((first_term, second_term), 'gy'), 'gx')]
  transfers between devices with their start and end apart: 28 -> 28, of which waited for: 5 -> 5; matrix products, arithmetic and copies ran while one was open for 35% -> 37% of each run, Pallas kernels for 0% -> 0%
where the time goes in v1:
time: 497 us; the launch traced here: 494 us
  other arithmetic  154 us (31%)
  local copies, waits for them, and re-layouts  138 us (28%)
  blocking collectives  105 us (21%)
  starting transfers between devices  76.3 us (15%)
  between operations  10.6 us (2%)
  waiting for transfers between devices  9.83 us (2%)
    psum x4, blocking collectives, sum_pairs(): return lax.psum(lax.psum((first_term, second_term), 'gy'), 'gx')  105 us
    scatter-add x3, other arithmetic, spread(): loads = jnp.zeros((6, seg_rows), jnp.float32).at[:, all_rows].add(pushes)  101 us
    gather x8, local copies, waits for them, and re-layouts, picked(): taken = jnp.take(source, all_rows, axis=1)  91.8 us
    ppermute x28, starting transfers between devices, passed_along(): return lax.ppermute(shard, axis, pairs)  76.3 us
    scatter-add x3, other arithmetic, spread(): jnp.zeros((6, 4 * export_cap), jnp.float32).at[:, slot_flat].add(cross_two)  18.5 us
    gather x8, local copies, waits for them, and re-layouts, incoming(): return jnp.take(flattened, slot_flat, axis=1)  12.5 us
    scatter-add x3, other arithmetic, spread(): loads.at[:, export_flat].add(jnp.moveaxis(returned, 0, 1).reshape(6, -1))  11.7 us
  transfers between devices with their start and end apart: 28, of which 5 were waited for; matrix products, arithmetic and copies ran while one was open for 37% of the time, Pallas kernels for 0%

profile of v1, /device:TPU:1, one launch (start us, length us, event | category | flops | bytes accessed | tf_op | source)
XLA Modules:
  0.0 493.5 jit_solution(9852824434111863647)
XLA Ops:
  11.4 3.3 collective-permute-start
  14.7 1.3 collective-permute-start.1
  16.0 1.3 collective-permute-start.2
  17.3 1.3 collective-permute-start.3
  19.2 1.9 collective-permute-start.4
  23.0 20.9 %gather_fusion.1 = f32[6144,6]{1,0:T(8,128)} fusion(f32[6,2048]{0,1:T(8,128)S(1)} %copy.319, s32[6144]{0:T(1024)S(1)} %fusion.33), kind=kCustom, calls=%fused_computation.3.clone | custom fusion | bytes 319488 | tf_op jit(solution)/shard_map/jit(_take)/gather | solution.py:121
  43.9 20.9 %gather_fusion = f32[6144,6]{1,0:T(8,128)} fusion(f32[6,2048]{0,1:T(8,128)S(1)} %copy.317, s32[6144]{0:T(1024)S(1)} %fusion.33), kind=kCustom, calls=%fused_computation.clone | custom fusion | bytes 319488 | tf_op jit(solution)/shard_map/jit(_take)/gather | solution.py:121
  66.0 2.4 copy.320
  72.4 1.9 slice_reduce_fusion.1
  75.3 1.3 reshape_dynamic-update-slice_fusion
  88.5 3.3 gather_fusion.3
  92.7 1.6 collective-permute-done.7
  94.6 2.8 gather_fusion.5
  100.2 6.1 %scatter_custom_fusion.1 = f32[6,512]{0,1:T(8,128)S(1)} fusion(s32[1024]{0:T(1024)S(1)} %bitcast.296, f32[1024,6]{1,0:T(8,128)S(1)} %copy.336, f32[]{:T(128)} %constant.32.clone.1), kind=kCustom, calls=%fused_computation.39 | custom fusion | flops 6144 | bytes 12292 | tf_op jit(solution)/shard_map/scatter-add | solution.py:153
  106.4 4.1 collective-permute-start.8
  110.4 5.0 %collective-permute-start.9 = (f32[6,128]{1,0:T(8,128)S(1)}, f32[6,128]{1,0:T(8,128)S(1)}, u32[]{:S(2)}, u32[]{:S(2)}) collective-permute-start(f32[6,128]{1,0:T(8,128)S(1)} %get-tuple-element.136), channel_id=1, source_target_pairs={{0,9},{1,10},{2,11},{3,12},{4,13},{5,14},{6,15},{7,16},{8,17},{9,1... | collective-permute-start | bytes 9224 | tf_op jit(solution)/shard_map/ppermute | solution.py:14
  115.5 5.1 %collective-permute-start.10 = (f32[6,128]{1,0:T(8,128)S(1)}, f32[6,128]{1,0:T(8,128)S(1)}, u32[]{:S(2)}, u32[]{:S(2)}) collective-permute-start(f32[6,128]{1,0:T(8,128)S(1)} %get-tuple-element.135), channel_id=1, source_target_pairs={{0,8},{1,9},{2,10},{3,11},{4,12},{5,13},{6,14},{7,15},{8,16},{9,17... | collective-permute-start | bytes 9224 | tf_op jit(solution)/shard_map/ppermute | solution.py:14
  120.6 6.2 %collective-permute-start.11 = (f32[6,128]{1,0:T(8,128)S(1)}, f32[6,128]{1,0:T(8,128)S(1)}, u32[]{:S(2)}, u32[]{:S(2)}) collective-permute-start(f32[6,128]{1,0:T(8,128)S(1)} %get-tuple-element.134), channel_id=1, source_target_pairs={{0,7},{1,8},{2,9},{3,10},{4,11},{5,12},{6,13},{7,14},{8,15},{9,16}... | collective-permute-start | bytes 9224 | tf_op jit(solution)/shard_map/ppermute | solution.py:14
  128.0 2.2 copy.335
  130.8 33.7 %scatter_custom_fusion = f32[6,2048]{0,1:T(8,128)S(1)} fusion(s32[6144]{0:T(1024)S(1)} %bitcast.275, f32[6144,6]{1,0:T(8,128)} %copy.335, f32[]{:T(128)} %constant.32.clone.1), kind=kCustom, calls=%fused_computation.25 | custom fusion | flops 36864 | bytes 49664 | tf_op jit(solution)/shard_map/scatter-add | solution.py:156
  164.9 3.9 scatter_fusion
  171.5 20.9 %gather_fusion.6 = f32[6144,6]{1,0:T(8,128)} fusion(f32[6,2048]{0,1:T(8,128)S(1)} %copy.344, s32[6144]{0:T(1024)S(1)} %copy-done.4), kind=kCustom, calls=%fused_computation.4.clone | custom fusion | bytes 319488 | tf_op jit(solution)/shard_map/jit(_take)/gather | solution.py:121
  192.6 3.2 collective-permute-start.12
  199.7 2.4 copy.345
  204.0 4.1 collective-permute-done.15
  208.3 2.8 gather_fusion.8
  215.3 11.1 %all-reduce.3 = (f32[]{:T(128)}, f32[]{:T(128)}) all-reduce(f32[]{:T(128)S(6)} %add.318, f32[]{:T(128)S(6)} %add.327), channel_id=1, replica_groups=mesh['gx'=16,'gy'=8] {'gy'}, use_global_device_ids=true, to_apply=%region_11.15 | all-reduce | flops 2 | bytes 16 | tf_op jit(solution)/shard_map/psum | solution.py:80
  226.4 43.8 %all-reduce.1 = (f32[]{:T(128)}, f32[]{:T(128)}) all-reduce(f32[]{:T(128)} %get-tuple-element.52, f32[]{:T(128)} %get-tuple-element.53), channel_id=1, replica_groups=mesh['gx'=16,'gy'=8] {'gx'}, use_global_device_ids=true, to_apply=%region_12.16 | all-reduce | flops 2 | bytes 16 | tf_op jit(solution)/shard_map/psum | solution.py:80
  271.8 6.2 %scatter_custom_fusion.4 = f32[6,512]{0,1:T(8,128)S(1)} fusion(s32[1024]{0:T(1024)} %bitcast.297, f32[1024,6]{1,0:T(8,128)S(1)} %copy.354, f32[]{:T(128)} %constant.32.clone.1), kind=kCustom, calls=%fused_computation.37 | custom fusion | flops 6144 | bytes 12800 | tf_op jit(solution)/shard_map/scatter-add | solution.py:153
  278.1 7.8 %collective-permute-start.16 = (f32[6,128]{1,0:T(8,128)S(1)}, f32[6,128]{1,0:T(8,128)S(1)}, u32[]{:S(2)}, u32[]{:S(2)}) collective-permute-start(f32[6,128]{1,0:T(8,128)S(1)} %get-tuple-element.123), channel_id=1, source_target_pairs={{0,1},{1,2},{2,3},{3,4},{4,5},{5,6},{6,7},{7,8},{8,9},{9,10},{10,1... | collective-permute-start | bytes 9224 | tf_op jit(solution)/shard_map/ppermute | solution.py:14
  288.5 3.3 collective-permute-start.19
  292.1 2.2 copy.353
  294.3 33.7 %scatter_custom_fusion.3 = f32[6,2048]{0,1:T(8,128)S(1)} fusion(s32[6144]{0:T(1024)} %bitcast.276, f32[6144,6]{1,0:T(8,128)} %copy.353, f32[]{:T(128)} %constant.32.clone.1), kind=kCustom, calls=%fused_computation.23 | custom fusion | flops 36864 | bytes 49664 | tf_op jit(solution)/shard_map/scatter-add | solution.py:156
  328.3 3.9 scatter_fusion.1
  333.9 20.9 %gather_fusion.9 = f32[6144,6]{1,0:T(8,128)} fusion(f32[6,2048]{0,1:T(8,128)S(1)} %copy.362, s32[6144]{0:T(1024)S(1)} %copy-done.4), kind=kCustom, calls=%fused_computation.5.clone | custom fusion | bytes 319488 | tf_op jit(solution)/shard_map/jit(_take)/gather | solution.py:121
  356.1 2.4 copy.363
  358.9 4.4 collective-permute-start.20
  369.1 2.5 collective-permute-done.23
  371.8 2.8 gather_fusion.11
  378.2 12.1 %all-reduce.2 = (f32[]{:T(128)}, f32[]{:T(128)}) all-reduce(f32[]{:T(128)S(6)} %add.329, f32[]{:T(128)S(6)} %add.336), channel_id=1, replica_groups=mesh['gx'=16,'gy'=8] {'gy'}, use_global_device_ids=true, to_apply=%region_29.33 | all-reduce | flops 2 | bytes 16 | tf_op jit(solution)/shard_map/psum | solution.py:80
  390.3 37.9 %all-reduce = (f32[]{:T(128)}, f32[]{:T(128)}) all-reduce(f32[]{:T(128)} %get-tuple-element.50, f32[]{:T(128)} %get-tuple-element.51), channel_id=1, replica_groups=mesh['gx'=16,'gy'=8] {'gx'}, use_global_device_ids=true, to_apply=%region_30.34 | all-reduce | flops 2 | bytes 16 | tf_op jit(solution)/shard_map/psum | solution.py:80
  430.4 6.2 %scatter_custom_fusion.7 = f32[6,512]{0,1:T(8,128)S(1)} fusion(s32[1024]{0:T(1024)} %bitcast.298, f32[1024,6]{1,0:T(8,128)S(1)} %copy.372, f32[]{:T(128)} %constant.32.clone.1), kind=kCustom, calls=%fused_computation.35 | custom fusion | flops 6144 | bytes 12800 | tf_op jit(solution)/shard_map/scatter-add | solution.py:153
  436.7 8.0 %collective-permute-start.24 = (f32[6,128]{1,0:T(8,128)S(1)}, f32[6,128]{1,0:T(8,128)S(1)}, u32[]{:S(2)}, u32[]{:S(2)}) collective-permute-start(f32[6,128]{1,0:T(8,128)S(1)} %get-tuple-element.113), channel_id=1, source_target_pairs={{0,1},{1,2},{2,3},{3,4},{4,5},{5,6},{6,7},{7,8},{8,9},{9,10},{10,1... | collective-permute-start | bytes 9224 | tf_op jit(solution)/shard_map/ppermute | solution.py:14
  446.0 2.0 collective-permute-start.26
  447.9 2.6 collective-permute-start.27
  451.5 2.2 copy.371
  453.7 33.7 %scatter_custom_fusion.6 = f32[6,2048]{0,1:T(8,128)S(1)} fusion(s32[6144]{0:T(1024)} %bitcast.277, f32[6144,6]{1,0:T(8,128)} %copy.371, f32[]{:T(128)} %constant.32.clone.1), kind=kCustom, calls=%fused_computation.21 | custom fusion | flops 36864 | bytes 49664 | tf_op jit(solution)/shard_map/scatter-add | solution.py:156
  487.8 4.0 scatter_fusion.2
  (381 shorter events, 65.4 us)
Async XLA Ops:
  2.1 62.7 %copy-start.73 = (pred[4,128]{1,0:T(4,128)(4,1)}, pred[4,128]{1,0:T(4,128)(4,1)S(1)}, u32[]{:S(2)}) copy-start(pred[4,128]{1,0:T(4,128)(4,1)S(1)} %compare_and_fusion.2) | copy-start | bytes 1540
  7.2 58.2 %copy-start.56 = (s32[1024]{0:T(1024)}, s32[1024]{0:T(1024)S(1)}, u32[]{:S(2)}) copy-start(s32[1024]{0:T(1024)S(1)} %pad_clamp_fusion) | copy-start | bytes 12292
  11.4 70.4 %collective-permute-start = (f32[6,128]{1,0:T(8,128)}, f32[6,128]{1,0:T(8,128)}, u32[]{:S(2)}, u32[]{:S(2)}) collective-permute-start(f32[6,128]{1,0:T(8,128)} %get-tuple-element.145), channel_id=1, source_target_pairs={{1,0},{2,1},{3,2},{4,3},{5,4},{6,5},{7,6},{8,7},{9,8},{10,9},{11,1... | collective-permute-start | bytes 9224 | tf_op jit(solution)/shard_map/ppermute | solution.py:14
  14.7 69.1 %collective-permute-start.1 = (f32[6,128]{1,0:T(8,128)}, f32[6,128]{1,0:T(8,128)}, u32[]{:S(2)}, u32[]{:S(2)}) collective-permute-start(f32[6,128]{1,0:T(8,128)} %get-tuple-element.148), channel_id=1, source_target_pairs={{9,0},{10,1},{11,2},{12,3},{13,4},{14,5},{15,6},{16,7},{17,8},{18,... | collective-permute-start | bytes 9224 | tf_op jit(solution)/shard_map/ppermute | solution.py:14
  16.0 69.7 %collective-permute-start.2 = (f32[6,128]{1,0:T(8,128)}, f32[6,128]{1,0:T(8,128)}, u32[]{:S(2)}, u32[]{:S(2)}) collective-permute-start(f32[6,128]{1,0:T(8,128)} %get-tuple-element.147), channel_id=1, source_target_pairs={{8,0},{9,1},{10,2},{11,3},{12,4},{13,5},{14,6},{15,7},{16,8},{17,9... | collective-permute-start | bytes 9224 | tf_op jit(solution)/shard_map/ppermute | solution.py:14
  17.3 70.4 %collective-permute-start.3 = (f32[6,128]{1,0:T(8,128)}, f32[6,128]{1,0:T(8,128)}, u32[]{:S(2)}, u32[]{:S(2)}) collective-permute-start(f32[6,128]{1,0:T(8,128)} %get-tuple-element.146), channel_id=1, source_target_pairs={{7,0},{8,1},{9,2},{10,3},{11,4},{12,5},{13,6},{14,7},{15,8},{16,9}... | collective-permute-start | bytes 9224 | tf_op jit(solution)/shard_map/ppermute | solution.py:14
  19.2 72.9 %collective-permute-start.4 = (f32[6,128]{1,0:T(8,128)}, f32[6,128]{1,0:T(8,128)}, u32[]{:S(2)}, u32[]{:S(2)}) collective-permute-start(f32[6,128]{1,0:T(8,128)} %get-tuple-element.141), channel_id=1, source_target_pairs={{1,0},{2,1},{3,2},{4,3},{5,4},{6,5},{7,6},{8,7},{9,8},{10,9},{11,1... | collective-permute-start | bytes 9224 | tf_op jit(solution)/shard_map/ppermute | solution.py:14
  78.7 52.1 %copy-start.61 = (s32[6144,1]{0,1:T(1,128)}, s32[6144,1]{0,1:T(1,128)S(1)}, u32[]{:S(2)}) copy-start(s32[6144,1]{0,1:T(1,128)S(1)} %compare_select_fusion) | copy-start | bytes 73732
  78.7 51.5 %copy-start.76 = (s32[1024,1]{0,1:T(1,128)}, s32[1024,1]{0,1:T(1,128)S(1)}, u32[]{:S(2)}) copy-start(s32[1024,1]{0,1:T(1,128)S(1)} %compare_select_fusion.2) | copy-start | bytes 12292
  80.3 84.6 %copy-start.58 = (s32[512,1]{0,1:T(1,128)}, s32[512,1]{0,1:T(1,128)S(1)}, u32[]{:S(2)}) copy-start(s32[512,1]{0,1:T(1,128)S(1)} %compare_select_fusion.3) | copy-start | bytes 6148
  81.7 48.5 %copy-start.38 = (f32[1,2,4,128]{3,1,2,0:T(2,128)}, f32[1,2,4,128]{3,1,2,0:T(2,128)S(1)}, u32[]{:S(2)}) copy-start(f32[1,2,4,128]{3,1,2,0:T(2,128)S(1)} %copy.396) | copy-start | bytes 12292
  81.7 11.0 %collective-permute-start.5 = (f32[6,128]{1,0:T(8,128)}, f32[6,128]{1,0:T(8,128)S(1)}, u32[]{:S(2)}, u32[]{:S(2)}) collective-permute-start(f32[6,128]{1,0:T(8,128)} %get-tuple-element.144), channel_id=1, source_target_pairs={{9,0},{10,1},{11,2},{12,3},{13,4},{14,5},{15,6},{16,7},{17,8},{18,... | collective-permute-start | bytes 9224 | tf_op jit(solution)/shard_map/ppermute | solution.py:14
  83.7 9.0 %collective-permute-start.6 = (f32[6,128]{1,0:T(8,128)}, f32[6,128]{1,0:T(8,128)S(1)}, u32[]{:S(2)}, u32[]{:S(2)}) collective-permute-start(f32[6,128]{1,0:T(8,128)} %get-tuple-element.143), channel_id=1, source_target_pairs={{8,0},{9,1},{10,2},{11,3},{12,4},{13,5},{14,6},{15,7},{16,8},{17,9... | collective-permute-start | bytes 9224 | tf_op jit(solution)/shard_map/ppermute | solution.py:14
  85.7 8.7 %collective-permute-start.7 = (f32[6,128]{1,0:T(8,128)}, f32[6,128]{1,0:T(8,128)S(1)}, u32[]{:S(2)}, u32[]{:S(2)}) collective-permute-start(f32[6,128]{1,0:T(8,128)} %get-tuple-element.142), channel_id=1, source_target_pairs={{7,0},{8,1},{9,2},{10,3},{11,4},{12,5},{13,6},{14,7},{15,8},{16,9}... | collective-permute-start | bytes 9224 | tf_op jit(solution)/shard_map/ppermute | solution.py:14
  98.8 65.8 %copy-start.9 = (f32[1,1024]{1,0:T(1,128)}, f32[1,1024]{1,0:T(1,128)S(1)}, u32[]{:S(2)}) copy-start(f32[1,1024]{1,0:T(1,128)S(1)} %get-tuple-element.110) | copy-start | bytes 12292
  98.8 65.8 %copy-start.12 = (f32[1,1024]{1,0:T(1,128)}, f32[1,1024]{1,0:T(1,128)S(1)}, u32[]{:S(2)}) copy-start(f32[1,1024]{1,0:T(1,128)S(1)} %get-tuple-element.111) | copy-start | bytes 12292
  98.8 65.8 %copy-start.15 = (f32[1,1024]{1,0:T(1,128)}, f32[1,1024]{1,0:T(1,128)S(1)}, u32[]{:S(2)}) copy-start(f32[1,1024]{1,0:T(1,128)S(1)} %get-tuple-element.112) | copy-start | bytes 12292
  106.4 58.2 %collective-permute-start.8 = (f32[6,128]{1,0:T(8,128)S(1)}, f32[6,128]{1,0:T(8,128)S(1)}, u32[]{:S(2)}, u32[]{:S(2)}) collective-permute-start(f32[6,128]{1,0:T(8,128)S(1)} %get-tuple-element.133), channel_id=1, source_target_pairs={{0,1},{1,2},{2,3},{3,4},{4,5},{5,6},{6,7},{7,8},{8,9},{9,10},{10,1... | collective-permute-start | bytes 9224 | tf_op jit(solution)/shard_map/ppermute | solution.py:14
  110.4 54.2 %collective-permute-start.9 = (f32[6,128]{1,0:T(8,128)S(1)}, f32[6,128]{1,0:T(8,128)S(1)}, u32[]{:S(2)}, u32[]{:S(2)}) collective-permute-start(f32[6,128]{1,0:T(8,128)S(1)} %get-tuple-element.136), channel_id=1, source_target_pairs={{0,9},{1,10},{2,11},{3,12},{4,13},{5,14},{6,15},{7,16},{8,17},{9,1... | collective-permute-start | bytes 9224 | tf_op jit(solution)/shard_map/ppermute | solution.py:14
  115.5 49.2 %collective-permute-start.10 = (f32[6,128]{1,0:T(8,128)S(1)}, f32[6,128]{1,0:T(8,128)S(1)}, u32[]{:S(2)}, u32[]{:S(2)}) collective-permute-start(f32[6,128]{1,0:T(8,128)S(1)} %get-tuple-element.135), channel_id=1, source_target_pairs={{0,8},{1,9},{2,10},{3,11},{4,12},{5,13},{6,14},{7,15},{8,16},{9,17... | collective-permute-start | bytes 9224 | tf_op jit(solution)/shard_map/ppermute | solution.py:14
  120.6 44.1 %collective-permute-start.11 = (f32[6,128]{1,0:T(8,128)S(1)}, f32[6,128]{1,0:T(8,128)S(1)}, u32[]{:S(2)}, u32[]{:S(2)}) collective-permute-start(f32[6,128]{1,0:T(8,128)S(1)} %get-tuple-element.134), channel_id=1, source_target_pairs={{0,7},{1,8},{2,9},{3,10},{4,11},{5,12},{6,13},{7,14},{8,15},{9,16}... | collective-permute-start | bytes 9224 | tf_op jit(solution)/shard_map/ppermute | solution.py:14
  192.6 11.0 %collective-permute-start.12 = (f32[6,128]{1,0:T(8,128)S(1)}, f32[6,128]{1,0:T(8,128)S(1)}, u32[]{:S(2)}, u32[]{:S(2)}) collective-permute-start(f32[6,128]{1,0:T(8,128)S(1)} %get-tuple-element.129), channel_id=1, source_target_pairs={{1,0},{2,1},{3,2},{4,3},{5,4},{6,5},{7,6},{8,7},{9,8},{10,9},{11,1... | collective-permute-start | bytes 9224 | tf_op jit(solution)/shard_map/ppermute | solution.py:14
  195.8 7.8 %collective-permute-start.13 = (f32[6,128]{1,0:T(8,128)S(1)}, f32[6,128]{1,0:T(8,128)S(1)}, u32[]{:S(2)}, u32[]{:S(2)}) collective-permute-start(f32[6,128]{1,0:T(8,128)S(1)} %get-tuple-element.132), channel_id=1, source_target_pairs={{9,0},{10,1},{11,2},{12,3},{13,4},{14,5},{15,6},{16,7},{17,8},{18,... | collective-permute-start | bytes 9224 | tf_op jit(solution)/shard_map/ppermute | solution.py:14
  197.1 6.9 %collective-permute-start.14 = (f32[6,128]{1,0:T(8,128)S(1)}, f32[6,128]{1,0:T(8,128)S(1)}, u32[]{:S(2)}, u32[]{:S(2)}) collective-permute-start(f32[6,128]{1,0:T(8,128)S(1)} %get-tuple-element.131), channel_id=1, source_target_pairs={{8,0},{9,1},{10,2},{11,3},{12,4},{13,5},{14,6},{15,7},{16,8},{17,9... | collective-permute-start | bytes 9224 | tf_op jit(solution)/shard_map/ppermute | solution.py:14
  198.4 93.4 %copy-start.49 = (f32[1,2560]{1,0:T(1,128)S(1)}, f32[1,2560]{1,0:T(1,128)}, u32[]{:S(2)}) copy-start(f32[1,2560]{1,0:T(1,128)} %get-tuple-element.65) | copy-start | bytes 30724
  198.4 9.7 %collective-permute-start.15 = (f32[6,128]{1,0:T(8,128)S(1)}, f32[6,128]{1,0:T(8,128)S(1)}, u32[]{:S(2)}, u32[]{:S(2)}) collective-permute-start(f32[6,128]{1,0:T(8,128)S(1)} %get-tuple-element.130), channel_id=1, source_target_pairs={{7,0},{8,1},{9,2},{10,3},{11,4},{12,5},{13,6},{14,7},{15,8},{16,9}... | collective-permute-start | bytes 9224 | tf_op jit(solution)/shard_map/ppermute | solution.py:14
  271.8 56.5 %copy-start.59 = (s32[512,1]{0,1:T(1,128)S(1)}, s32[512,1]{0,1:T(1,128)}, u32[]{:S(2)}) copy-start(s32[512,1]{0,1:T(1,128)} %copy-done.58) | copy-start | bytes 6148
  278.1 49.9 %collective-permute-start.16 = (f32[6,128]{1,0:T(8,128)S(1)}, f32[6,128]{1,0:T(8,128)S(1)}, u32[]{:S(2)}, u32[]{:S(2)}) collective-permute-start(f32[6,128]{1,0:T(8,128)S(1)} %get-tuple-element.123), channel_id=1, source_target_pairs={{0,1},{1,2},{2,3},{3,4},{4,5},{5,6},{6,7},{7,8},{8,9},{9,10},{10,1... | collective-permute-start | bytes 9224 | tf_op jit(solution)/shard_map/ppermute | solution.py:14
  285.9 42.1 %collective-permute-start.17 = (f32[6,128]{1,0:T(8,128)S(1)}, f32[6,128]{1,0:T(8,128)S(1)}, u32[]{:S(2)}, u32[]{:S(2)}) collective-permute-start(f32[6,128]{1,0:T(8,128)S(1)} %get-tuple-element.126), channel_id=1, source_target_pairs={{0,9},{1,10},{2,11},{3,12},{4,13},{5,14},{6,15},{7,16},{8,17},{9,1... | collective-permute-start | bytes 9224 | tf_op jit(solution)/shard_map/ppermute | solution.py:14
  287.2 40.8 %collective-permute-start.18 = (f32[6,128]{1,0:T(8,128)S(1)}, f32[6,128]{1,0:T(8,128)S(1)}, u32[]{:S(2)}, u32[]{:S(2)}) collective-permute-start(f32[6,128]{1,0:T(8,128)S(1)} %get-tuple-element.125), channel_id=1, source_target_pairs={{0,8},{1,9},{2,10},{3,11},{4,12},{5,13},{6,14},{7,15},{8,16},{9,17... | collective-permute-start | bytes 9224 | tf_op jit(solution)/shard_map/ppermute | solution.py:14
  288.5 39.6 %collective-permute-start.19 = (f32[6,128]{1,0:T(8,128)S(1)}, f32[6,128]{1,0:T(8,128)S(1)}, u32[]{:S(2)}, u32[]{:S(2)}) collective-permute-start(f32[6,128]{1,0:T(8,128)S(1)} %get-tuple-element.124), channel_id=1, source_target_pairs={{0,7},{1,8},{2,9},{3,10},{4,11},{5,12},{6,13},{7,14},{8,15},{9,16}... | collective-permute-start | bytes 9224 | tf_op jit(solution)/shard_map/ppermute | solution.py:14
  333.9 37.8 %copy-start.37 = (s32[1024]{0:T(1024)S(1)}, s32[1024]{0:T(1024)}, u32[]{:S(2)}) copy-start(s32[1024]{0:T(1024)} %broadcast_clamp_fusion) | copy-start | bytes 12292
  356.1 94.5 %copy-start.50 = (f32[1,2560]{1,0:T(1,128)S(1)}, f32[1,2560]{1,0:T(1,128)}, u32[]{:S(2)}) copy-start(f32[1,2560]{1,0:T(1,128)} %get-tuple-element.65) | copy-start | bytes 30724
  356.1 94.5 %copy-start.55 = (f32[1,2560]{1,0:T(1,128)S(1)}, f32[1,2560]{1,0:T(1,128)}, u32[]{:S(2)}) copy-start(f32[1,2560]{1,0:T(1,128)} %get-tuple-element.66) | copy-start | bytes 30724
  358.5 92.3 %copy-start.66 = (f32[1,4,256]{2,1,0:T(4,128)S(1)}, f32[1,4,256]{2,1,0:T(4,128)}, u32[]{:S(2)}) copy-start(f32[1,4,256]{2,1,0:T(4,128)} %sub.334) | copy-start | bytes 12292
  358.5 92.3 %copy-start.67 = (f32[1,4,256]{2,1,0:T(4,128)S(1)}, f32[1,4,256]{2,1,0:T(4,128)}, u32[]{:S(2)}) copy-start(f32[1,4,256]{2,1,0:T(4,128)} %sqrt.64) | copy-start | bytes 12292
  358.5 92.3 %copy-start.68 = (f32[1,4,256]{2,1,0:T(4,128)S(1)}, f32[1,4,256]{2,1,0:T(4,128)}, u32[]{:S(2)}) copy-start(f32[1,4,256]{2,1,0:T(4,128)} %squeeze.193) | copy-start | bytes 12292
  358.5 92.3 %copy-start.69 = (f32[1,4,256]{2,1,0:T(4,128)S(1)}, f32[1,4,256]{2,1,0:T(4,128)}, u32[]{:S(2)}) copy-start(f32[1,4,256]{2,1,0:T(4,128)} %squeeze.194) | copy-start | bytes 12292
  358.5 92.3 %copy-start.77 = (s32[1,4]{1,0:T(1,128)S(1)}, s32[1,4]{1,0:T(1,128)}, u32[]{:S(2)}) copy-start(s32[1,4]{1,0:T(1,128)} %param.40) | copy-start | bytes 52
  358.9 9.0 %collective-permute-start.20 = (f32[6,128]{1,0:T(8,128)S(1)}, f32[6,128]{1,0:T(8,128)S(1)}, u32[]{:S(2)}, u32[]{:S(2)}) collective-permute-start(f32[6,128]{1,0:T(8,128)S(1)} %get-tuple-element.119), channel_id=1, source_target_pairs={{1,0},{2,1},{3,2},{4,3},{5,4},{6,5},{7,6},{8,7},{9,8},{10,9},{11,1... | collective-permute-start | bytes 9224 | tf_op jit(solution)/shard_map/ppermute | solution.py:14
  363.3 5.8 %collective-permute-start.21 = (f32[6,128]{1,0:T(8,128)S(1)}, f32[6,128]{1,0:T(8,128)S(1)}, u32[]{:S(2)}, u32[]{:S(2)}) collective-permute-start(f32[6,128]{1,0:T(8,128)S(1)} %get-tuple-element.122), channel_id=1, source_target_pairs={{9,0},{10,1},{11,2},{12,3},{13,4},{14,5},{15,6},{16,7},{17,8},{18,... | collective-permute-start | bytes 9224 | tf_op jit(solution)/shard_map/ppermute | solution.py:14
  364.6 4.5 collective-permute-start.22
  365.9 5.7 %collective-permute-start.23 = (f32[6,128]{1,0:T(8,128)S(1)}, f32[6,128]{1,0:T(8,128)S(1)}, u32[]{:S(2)}, u32[]{:S(2)}) collective-permute-start(f32[6,128]{1,0:T(8,128)S(1)} %get-tuple-element.120), channel_id=1, source_target_pairs={{7,0},{8,1},{9,2},{10,3},{11,4},{12,5},{13,6},{14,7},{15,8},{16,9}... | collective-permute-start | bytes 9224 | tf_op jit(solution)/shard_map/ppermute | solution.py:14
  430.4 57.4 %copy-start.60 = (s32[512,1]{0,1:T(1,128)S(1)}, s32[512,1]{0,1:T(1,128)}, u32[]{:S(2)}) copy-start(s32[512,1]{0,1:T(1,128)} %copy-done.58) | copy-start | bytes 6148
  436.7 50.8 %collective-permute-start.24 = (f32[6,128]{1,0:T(8,128)S(1)}, f32[6,128]{1,0:T(8,128)S(1)}, u32[]{:S(2)}, u32[]{:S(2)}) collective-permute-start(f32[6,128]{1,0:T(8,128)S(1)} %get-tuple-element.113), channel_id=1, source_target_pairs={{0,1},{1,2},{2,3},{3,4},{4,5},{5,6},{6,7},{7,8},{8,9},{9,10},{10,1... | collective-permute-start | bytes 9224 | tf_op jit(solution)/shard_map/ppermute | solution.py:14
  444.7 42.8 %collective-permute-start.25 = (f32[6,128]{1,0:T(8,128)S(1)}, f32[6,128]{1,0:T(8,128)S(1)}, u32[]{:S(2)}, u32[]{:S(2)}) collective-permute-start(f32[6,128]{1,0:T(8,128)S(1)} %get-tuple-element.116), channel_id=1, source_target_pairs={{0,9},{1,10},{2,11},{3,12},{4,13},{5,14},{6,15},{7,16},{8,17},{9,1... | collective-permute-start | bytes 9224 | tf_op jit(solution)/shard_map/ppermute | solution.py:14
  446.0 41.6 %collective-permute-start.26 = (f32[6,128]{1,0:T(8,128)S(1)}, f32[6,128]{1,0:T(8,128)S(1)}, u32[]{:S(2)}, u32[]{:S(2)}) collective-permute-start(f32[6,128]{1,0:T(8,128)S(1)} %get-tuple-element.115), channel_id=1, source_target_pairs={{0,8},{1,9},{2,10},{3,11},{4,12},{5,13},{6,14},{7,15},{8,16},{9,17... | collective-permute-start | bytes 9224 | tf_op jit(solution)/shard_map/ppermute | solution.py:14
  447.9 39.6 %collective-permute-start.27 = (f32[6,128]{1,0:T(8,128)S(1)}, f32[6,128]{1,0:T(8,128)S(1)}, u32[]{:S(2)}, u32[]{:S(2)}) collective-permute-start(f32[6,128]{1,0:T(8,128)S(1)} %get-tuple-element.114), channel_id=1, source_target_pairs={{0,7},{1,8},{2,9},{3,10},{4,11},{5,12},{6,13},{7,14},{8,15},{9,16}... | collective-permute-start | bytes 9224 | tf_op jit(solution)/shard_map/ppermute | solution.py:14
  (58 other events, 992.8 us)
